TPU v7x, 32 devices: a whole 2x2x4 slice. The times are simulated.
32 devices in a mesh: region: 4 (over z), member: 8 (over y, x, core).
Axes of the slice: x: 2, y: 2, z: 4, core: 2. Of those that a mesh axis runs over, the one named last changes fastest.
Arguments:
- ensemble: float32 [256, 1024], P('member', 'region'), may hold values from -6 to 6
- obs_value: float32 [2048], replicated, may hold values from -6 to 6
- obs_error: float32 [2048], replicated, may hold values from 0.5 to 2
- obs_region: int32 [2048], replicated, may hold values from 0 to 3
- obs_cell: int32 [2048], replicated, may hold values from 0 to 255
- order: int32 [2048], replicated, may hold values from 0 to 2047, each once
- footprint: int32 [2, 8, 2], P(None, 'region'), may hold values from 0 to 15, as said below
Outputs:
- analysis: float32 [256, 1024], P('member', 'region')
Inputs may be any that keep to these rules, and one draw needn't show every extreme that they name: `footprint`: the 2 observation tiles listed for one state tile and batch are different.
All inputs are finite; a program needn't handle non-finite values.
Results may differ from a plain program's by a relative error of at most 0.0003.
Values sent between devices are 32-bit elements; how exact they have to be, the bound alone decides.
A program may use at most 64 MiB of HBM per device.

v0:
```python
import jax
import jax.numpy as jnp
from jax import lax
from jax.sharding import PartitionSpec as P

NOBS = 1024
BATCHES = 2
STILE = 128
OTILE = 64
FOOT = 2


def per_device(ensemble, obs_value, obs_error, obs_region, obs_cell, order, footprint):
    mem_dev, cell_count = ensemble.shape
    members = mem_dev * lax.axis_size("member")
    tile_count = cell_count // STILE
    state = ensemble
    region = lax.axis_index("region")
    offsets = jnp.arange(OTILE, dtype=jnp.int32)
    for batch_no in range(BATCHES):
        chosen = order[batch_no * NOBS : (batch_no + 1) * NOBS]
        owned_here = obs_region[chosen] == region
        picked = jnp.where(owned_here[None, :], jnp.take(state, obs_cell[chosen], axis=1), 0.0)
        priors = lax.psum(picked, "region")
        obs_index = (footprint[batch_no][:, :, None] * OTILE + offsets[None, None, :]).reshape(
            tile_count, FOOT * OTILE
        )
        state_tiles = state.reshape(mem_dev, tile_count, STILE)
        s_one = jnp.sum(priors, axis=0)
        s_two = jnp.sum(priors * priors, axis=0)
        s_one, s_two = lax.psum((s_one, s_two), "member")
        obs_mean = s_one / members
        obs_pert = priors - obs_mean[None, :]
        obs_tiles = jnp.take(obs_pert, obs_index, axis=1)
        partial_value = jnp.einsum(
            "mtj,mtc->tjc", obs_tiles, state_tiles, precision=lax.Precision.HIGHEST
        )
        summed = lax.psum(partial_value, "member")
        covariance = summed / (members - 1)
        obs_var = (s_two - s_one * obs_mean) / (members - 1)
        err_var = obs_error[chosen]
        obs_gain = 1.0 / (obs_var + err_var)
        shrink = 1.0 / (1.0 + jnp.sqrt(err_var * obs_gain))
        innovation = obs_value[chosen] - obs_mean
        weight = covariance * obs_gain[obs_index][:, :, None]
        mean_step = jnp.einsum(
            "tjc,tj->tc", weight, innovation[obs_index], precision=lax.Precision.HIGHEST
        )
        scaled = obs_tiles * shrink[obs_index][None, :, :]
        pert_step = jnp.einsum("mtj,tjc->mtc", scaled, weight, precision=lax.Precision.HIGHEST)
        state = (
            state + mean_step.reshape(cell_count)[None, :] - pert_step.reshape(mem_dev, cell_count)
        )
    return state


def solution(mesh):
    in_specs = (P("member", "region"), P(), P(), P(), P(), P(), P(None, "region", None))
    out_specs = P("member", "region")
    return jax.shard_map(
        per_device, mesh=mesh, in_specs=in_specs, out_specs=out_specs, check_vma=False
    )
```

profile of v0, /device:TPU:0, one launch (start us, length us, event | category | flops | bytes accessed | tf_op | source)
XLA Modules:
  0.0 252.9 jit_solution(2424373004848491540)
XLA Ops:
  7.3 6.2 %gather_fusion.1 = s32[1024]{0:T(1024)S(1)} fusion(s32[2048]{0:T(1024)S(1)} %copy-done, s32[1024]{0:T(1024)S(1)} %get-tuple-element.20), kind=kCustom, calls=%fused_computation.5 | custom fusion | bytes 12288 | tf_op jit(solution)/shard_map/gather | solution.py:23
  13.4 6.2 %gather_fusion = s32[1024]{0:T(1024)S(1)} fusion(s32[2048]{0:T(1024)S(1)} %copy-done.1, s32[1024]{0:T(1024)S(1)} %get-tuple-element.20), kind=kCustom, calls=%fused_computation.4 | custom fusion | bytes 12288 | tf_op jit(solution)/shard_map/gather | solution.py:22
  19.8 2.8 %gather_fusion.14 = f32[1024,32]{1,0:T(8,128)S(1)} fusion(f32[32,256]{0,1:T(8,128)S(1)} %copy.26, s32[1024]{0:T(1024)S(1)} %fusion.34), kind=kCustom, calls=%fused_computation.clone | custom fusion | bytes 266240 | tf_op jit(solution)/shard_map/jit(_take)/gather | solution.py:23
  22.6 1.1 bitcast_select_fusion.1
  25.0 6.1 %gather_fusion.8 = s32[1024]{0:T(1024)S(1)} fusion(s32[2048]{0:T(1024)S(1)} %copy-done, s32[1024]{0:T(1024)S(1)} %get-tuple-element.19), kind=kCustom, calls=%fused_computation.12 | custom fusion | bytes 12288 | tf_op jit(solution)/shard_map/gather | solution.py:23
  31.1 6.2 %gather_fusion.7 = s32[1024]{0:T(1024)S(1)} fusion(s32[2048]{0:T(1024)S(1)} %copy-done.1, s32[1024]{0:T(1024)S(1)} %get-tuple-element.19), kind=kCustom, calls=%fused_computation.11 | custom fusion | bytes 12288 | tf_op jit(solution)/shard_map/gather | solution.py:22
  38.0 6.1 %gather_fusion.2 = f32[1024]{0:T(1024)S(1)} fusion(f32[2048]{0:T(1024)S(1)} %copy-done.2, s32[1024]{0:T(1024)S(1)} %get-tuple-element.20), kind=kCustom, calls=%fused_computation.6 | custom fusion | bytes 12288 | tf_op jit(solution)/shard_map/gather | solution.py:41
  44.2 6.2 %gather_fusion.4 = f32[1024]{0:T(1024)S(1)} fusion(f32[2048]{0:T(1024)S(1)} %copy-done.3, s32[1024]{0:T(1024)S(1)} %get-tuple-element.20), kind=kCustom, calls=%fused_computation.8 | custom fusion | bytes 12288 | tf_op jit(solution)/shard_map/gather | solution.py:44
  50.4 14.5 %all-reduce.7.cloned.1.call-done = f32[32,1024]{0,1:T(8,128)} async-done(((f32[32,1024]{0,1:T(8,128)}), f32[32,1024]{0,1:T(8,128)}) %all-reduce.7.cloned.1.call-update) | async-done | bytes 131088 | tf_op jit(solution)/shard_map/psum | solution.py:24
  64.9 1.4 multiply_reduce_fusion.1
  66.3 13.2 %all-reduce.1 = (f32[1024]{0:T(1024)S(1)}, f32[1024]{0:T(1024)S(1)}) all-reduce(f32[1024]{0:T(1024)S(1)} %get-tuple-element.10, f32[1024]{0:T(1024)S(1)} %get-tuple-element.9), channel_id=1, replica_groups=mesh['region'=4,'member'=8] {'member'}, use_global_device_ids=true, to_apply=%region_2.4 | all-reduce | flops 2048 | bytes 16384 | tf_op jit(solution)/shard_map/psum | solution.py:31
  79.7 0.7 gather_fusion.15
  80.6 1.0 fusion.13
  81.7 1.4 gather_fusion.3
  83.1 1.4 gather_fusion.5
  84.4 1.4 gather_fusion.6
  85.8 46.9 %all-reduce.9.cloned.1.call-done = f32[2,128,128]{2,1,0:T(8,128)} async-done(((f32[2,128,128]{2,1,0:T(8,128)}), f32[2,128,128]{2,1,0:T(8,128)}) %all-reduce.9.cloned.1.call-update) | async-done | bytes 131088 | tf_op jit(solution)/shard_map/psum | solution.py:38
  132.7 1.3 fusion.4
  134.4 2.8 %gather_fusion.16 = f32[1024,32]{1,0:T(8,128)S(1)} fusion(f32[32,256]{0,1:T(8,128)S(1)} %copy.30, s32[1024]{0:T(1024)S(1)} %fusion.35), kind=kCustom, calls=%fused_computation.2.clone | custom fusion | bytes 266240 | tf_op jit(solution)/shard_map/jit(_take)/gather | solution.py:23
  137.3 1.1 bitcast_select_fusion
  138.5 6.2 %gather_fusion.9 = f32[1024]{0:T(1024)S(1)} fusion(f32[2048]{0:T(1024)S(1)} %copy-done.2, s32[1024]{0:T(1024)S(1)} %get-tuple-element.19), kind=kCustom, calls=%fused_computation.13 | custom fusion | bytes 12288 | tf_op jit(solution)/shard_map/gather | solution.py:41
  144.6 6.2 %gather_fusion.11 = f32[1024]{0:T(1024)S(1)} fusion(f32[2048]{0:T(1024)S(1)} %copy-done.3, s32[1024]{0:T(1024)S(1)} %get-tuple-element.19), kind=kCustom, calls=%fused_computation.15 | custom fusion | bytes 12288 | tf_op jit(solution)/shard_map/gather | solution.py:44
  150.8 25.4 %all-reduce.11.cloned.1.call-done = f32[32,1024]{0,1:T(8,128)} async-done(((f32[32,1024]{0,1:T(8,128)}), f32[32,1024]{0,1:T(8,128)}) %all-reduce.11.cloned.1.call-update) | async-done | bytes 131088 | tf_op jit(solution)/shard_map/psum | solution.py:24
  176.2 1.4 multiply_reduce_fusion
  177.7 13.2 %all-reduce = (f32[1024]{0:T(1024)S(1)}, f32[1024]{0:T(1024)S(1)}) all-reduce(f32[1024]{0:T(1024)S(1)} %get-tuple-element.8, f32[1024]{0:T(1024)S(1)} %get-tuple-element.6), channel_id=1, replica_groups=mesh['region'=4,'member'=8] {'member'}, use_global_device_ids=true, to_apply=%region_8.11 | all-reduce | flops 2048 | bytes 16384 | tf_op jit(solution)/shard_map/psum | solution.py:31
  191.1 0.7 gather_fusion.17
  191.9 1.0 fusion.10
  193.0 1.4 gather_fusion.10
  194.4 1.4 gather_fusion.12
  195.8 1.4 gather_fusion.13
  197.1 47.0 %all-reduce.13.cloned.1.call-done = f32[2,128,128]{2,1,0:T(8,128)} async-done(((f32[2,128,128]{2,1,0:T(8,128)}), f32[2,128,128]{2,1,0:T(8,128)}) %all-reduce.13.cloned.1.call-update) | async-done | bytes 131088 | tf_op jit(solution)/shard_map/psum | solution.py:38
  244.1 1.3 fusion.1
  (62 shorter events, 4.9 us)
Async XLA Ops:
  6.5 0.7 copy-start
  6.5 58.3 %all-reduce.7.cloned.1.call-start = ((), (), s32[]{:S(2)}) async-start(), calls=%async_computation | async-start | bytes 1048576 | tf_op jit(solution)/shard_map/psum | solution.py:24
  7.3 6.2 %copy-start.1 = (s32[2048]{0:T(1024)S(1)}, s32[2048]{0:T(1024)}, u32[]{:S(2)}) copy-start(s32[2048]{0:T(1024)} %param.14) | copy-start | bytes 24580
  13.4 6.2 %copy-start.8 = (f32[32,256]{1,0:T(8,128)S(1)}, f32[32,256]{1,0:T(8,128)}, u32[]{:S(2)}) copy-start(f32[32,256]{1,0:T(8,128)} %param.11) | copy-start | bytes 98308
  23.7 0.7 copy-start.9
  23.7 109.0 %all-reduce.9.cloned.1.call-start = ((), (), s32[]{:S(2)}) async-start(), calls=%async_computation.1 | async-start | bytes 262144 | tf_op jit(solution)/shard_map/psum | solution.py:38
  37.3 0.7 copy-start.2
  38.0 6.2 %copy-start.3 = (f32[2048]{0:T(1024)S(1)}, f32[2048]{0:T(1024)}, u32[]{:S(2)}) copy-start(f32[2048]{0:T(1024)} %param.12) | copy-start | bytes 24580
  64.9 14.7 %copy-start.4 = (f32[32,1024]{0,1:T(8,128)S(1)}, f32[32,1024]{0,1:T(8,128)}, u32[]{:S(2)}) copy-start(f32[32,1024]{0,1:T(8,128)} %all-reduce.7.cloned.1.call-done) | copy-start | bytes 393220
  81.6 94.6 %all-reduce.11.cloned.1.call-start = ((), (), s32[]{:S(2)}) async-start(), calls=%async_computation.2 | async-start | bytes 1048576 | tf_op jit(solution)/shard_map/psum | solution.py:24
  132.7 1.3 copy-start.6
  138.4 105.7 %all-reduce.13.cloned.1.call-start = ((), (), s32[]{:S(2)}) async-start(), calls=%async_computation.3 | async-start | bytes 262144 | tf_op jit(solution)/shard_map/psum | solution.py:38
  176.2 14.7 %copy-start.5 = (f32[32,1024]{0,1:T(8,128)S(1)}, f32[32,1024]{0,1:T(8,128)}, u32[]{:S(2)}) copy-start(f32[32,1024]{0,1:T(8,128)} %all-reduce.11.cloned.1.call-done) | copy-start | bytes 393220
  244.1 1.3 copy-start.7
Sparse Core Ops, SparseCore 0:
  23.9 40.9 all-reduce.6
  81.7 50.9 all-reduce.8
  138.6 37.6 all-reduce.10
  193.1 50.9 all-reduce.12
where the time goes:
time: 253 us
  waiting for transfers between devices  134 us (53%)
  local copies, waits for them, and re-layouts  66.7 us (26%)
  blocking collectives  26.3 us (10%)
  between operations  13.5 us (5%)
  other arithmetic  7.04 us (3%)
  matrix products  5.26 us (2%)
    psum x2, waiting for transfers between devices, per_device(): summed = lax.psum(partial_value, 'member')  93.9 us
    psum x2, waiting for transfers between devices, per_device(): priors = lax.psum(picked, 'region')  39.9 us
    psum x2, blocking collectives, per_device(): s_one, s_two = lax.psum((s_one, s_two), 'member')  26.3 us
    gather x2, local copies, waits for them, and re-layouts, per_device(): innovation = obs_value[chosen] - obs_mean  12.3 us
    gather x2, local copies, waits for them, and re-layouts, per_device(): owned_here = obs_region[chosen] == region  12.3 us
    gather x2, local copies, waits for them, and re-layouts, per_device(): obs_cell[chosen]  12.3 us
    gather x2, local copies, waits for them, and re-layouts, per_device(): err_var = obs_error[chosen]  12.3 us
    gather x2, local copies, waits for them, and re-layouts, per_device(): jnp.take(state, obs_cell[chosen], axis=1)  5.64 us
  transfers between devices with their start and end apart: 4, of which 4 were waited for; matrix products, arithmetic and copies ran while one was open for 18% of the time, Pallas kernels for 0%

commit v1 on v0

--- a/solution.py
+++ b/solution.py
@@ -1,6 +1,10 @@
+import functools
+
 import jax
 import jax.numpy as jnp
 from jax import lax
+from jax.experimental import pallas as pl
+from jax.experimental.pallas import tpu as pltpu
 from jax.sharding import PartitionSpec as P
 
 NOBS = 1024
@@ -8,9 +12,276 @@
 STILE = 128
 OTILE = 64
 FOOT = 2
-
-
-def per_device(ensemble, obs_value, obs_error, obs_region, obs_cell, order, footprint):
+CORES = 2
+LANES = 128
+MESH = pl.DeviceIdType.MESH
+F32 = jnp.float32
+BF16 = jnp.bfloat16
+REPLICATED_LIMIT = 4 * 1024 * 1024
+
+
+def split2(x):
+    hi = x.astype(BF16)
+    lo = (x - hi.astype(F32)).astype(BF16)
+    return hi, lo
+
+
+def split3(x):
+    hi = x.astype(BF16)
+    rest = x - hi.astype(F32)
+    mid = rest.astype(BF16)
+    lo = (rest - mid.astype(F32)).astype(BF16)
+    return hi.astype(F32), mid.astype(F32), lo.astype(F32)
+
+
+def dot(a, b, transposed=False):
+    dims = (((1,), (1 if transposed else 0,)), ((), ()))
+    return lax.dot_general(a, b, dims, preferred_element_type=F32)
+
+
+def dot3(a, b, transposed=False):
+    a_hi, a_lo = a
+    b_hi, b_lo = b
+    return dot(a_hi, b_hi, transposed) + (dot(a_hi, b_lo, transposed) + dot(a_lo, b_hi, transposed))
+
+
+def obs_terms(priors, err, val, members):
+    mean = jnp.sum(priors, axis=1, keepdims=True) * (1.0 / members)
+    pert = priors - mean
+    var = jnp.sum(pert * pert, axis=1, keepdims=True) * (1.0 / (members - 1))
+    gain = 1.0 / (var + err)
+    shrink = 1.0 / (1.0 + jnp.sqrt(err * gain))
+    step = (gain * (1.0 / (members - 1))) * ((val - mean) - shrink * pert)
+    return pert, step
+
+
+def kernel(
+    nr, nm, fp_ref, ens_ref, order_ref, region_ref, cell_ref, error_ref, value_ref, out_ref,
+    gathered, fp_all, fp_own, feat, hot, state_t, parts, pert_hi, pert_lo, step_hi, step_lo, final,
+    send_sem, recv_sem, fp_send, fp_recv,
+):
+    my_r, my_m = lax.axis_index("region"), lax.axis_index("member")
+    md, cd = ens_ref.shape
+    members, cells = md * nm, cd * nr
+    chips = nm // CORES
+    chip, core = my_m // CORES, my_m % CORES
+    mate = chip * CORES + (1 - core)
+    tiles_dev = cd // STILE
+    z_peers = [(my_r + d) % nr for d in range(1, nr)]
+    xy_peers = [((chip + e) % chips) * CORES + core for e in range(1, chips)]
+
+    barrier = pltpu.get_barrier_semaphore()
+    for r in z_peers:
+        pl.semaphore_signal(barrier, inc=1, device_id=(r, my_m), device_id_type=MESH)
+    for m in xy_peers + [mate]:
+        pl.semaphore_signal(barrier, inc=1, device_id=(my_r, m), device_id_type=MESH)
+    slots = BATCHES * tiles_dev * FOOT
+    lane8 = lax.broadcasted_iota(jnp.int32, (8, LANES), 1)
+    fp_sent, fp_here = [jnp.zeros((8, LANES), jnp.int32)] * 2
+    slot = 0
+    for b in range(BATCHES):
+        for t in range(tiles_dev):
+            for f in range(FOOT):
+                tile = fp_ref[b, t, f]
+                fp_sent = jnp.where(lane8 == my_r * slots + slot, tile, fp_sent)
+                fp_here = jnp.where(lane8 == nr * slots + slot, tile, fp_here)
+                slot += 1
+    fp_own[...] = fp_sent
+    pl.semaphore_wait(barrier, len(z_peers) + len(xy_peers) + 1)
+
+    sent = []
+
+    def block(r, m):
+        return gathered.at[r, pl.ds(pl.multiple_of(m * md, md), md), :]
+
+    def send(r, m, to, own=False):
+        copy = pltpu.make_async_remote_copy(
+            src_ref=ens_ref if own else block(r, m),
+            dst_ref=block(r, m),
+            send_sem=send_sem.at[len(sent)],
+            recv_sem=recv_sem.at[r, m],
+            device_id=to,
+            device_id_type=MESH,
+        )
+        copy.start()
+        sent.append(copy)
+
+    def arrived(r, m):
+        pltpu.make_async_remote_copy(
+            src_ref=block(r, m),
+            dst_ref=block(r, m),
+            send_sem=send_sem.at[0],
+            recv_sem=recv_sem.at[r, m],
+            device_id=(my_r, mate),
+            device_id_type=MESH,
+        ).wait_recv()
+
+    def fp_copy(i, r_from, r_to):
+        return pltpu.make_async_remote_copy(
+            src_ref=fp_own,
+            dst_ref=fp_all.at[r_from],
+            send_sem=fp_send.at[i],
+            recv_sem=fp_recv.at[r_from],
+            device_id=(r_to, my_m),
+            device_id_type=MESH,
+        )
+
+    for r in z_peers:
+        send(my_r, my_m, (r, my_m), own=True)
+    for m in xy_peers:
+        send(my_r, my_m, (my_r, m), own=True)
+    send(my_r, my_m, (my_r, mate), own=True)
+    for i, r in enumerate(z_peers):
+        fp_copy(i, my_r, r).start()
+    gathered[my_r, pl.ds(pl.multiple_of(my_m * md, md), md), :] = ens_ref[...]
+
+    rows = order_ref.shape[0]
+    table = jnp.concatenate(
+        [region_ref[...].astype(F32), cell_ref[...].astype(F32)]
+        + list(split3(error_ref[...]))
+        + list(split3(value_ref[...])),
+        axis=0,
+    )
+    table_t = jnp.transpose(table).astype(BF16)
+    width = table.shape[0]
+    order_t = jnp.transpose(
+        jnp.concatenate([order_ref[...].astype(F32), jnp.zeros((LANES - rows, LANES), F32)], axis=0)
+    ).astype(jnp.int32)
+    lane = lax.broadcasted_iota(jnp.int32, (LANES, LANES), 1)
+    line = lax.broadcasted_iota(jnp.int32, (LANES, LANES), 0)
+    wide_lane = lax.broadcasted_iota(jnp.int32, (LANES, width), 1)
+    kind = lax.broadcasted_iota(jnp.int32, (width, LANES), 0) // rows
+    column = lax.broadcasted_iota(jnp.int32, (width, LANES), 1)
+    collect = jnp.where((kind == 0) & (column == 0), float(cd), 0.0)
+    collect = jnp.where((kind == 1) & (column == 0), 1.0, collect)
+    collect = jnp.where((kind >= 2) & (kind <= 4) & (column == 1), 1.0, collect)
+    collect = jnp.where((kind >= 5) & (column == 2), 1.0, collect).astype(BF16)
+    for i, r in enumerate(z_peers):
+        fp_copy(i, r, r).wait_recv()
+        fp_here = fp_here + fp_all[r]
+    tile_of = (fp_here + fp_sent)[0:1, :]
+    lane1 = lax.broadcasted_iota(jnp.int32, (1, LANES), 1)
+    batch_of = lane1 % slots // (tiles_dev * FOOT)
+    half = LANES // OTILE
+    pick = jnp.where(line == batch_of * (NOBS // LANES) + tile_of // half, 1.0, 0.0).astype(BF16)
+    high_all = dot((order_t // LANES).astype(F32).astype(BF16), pick)
+    low_all = dot((order_t % LANES).astype(F32).astype(BF16), pick)
+    upper = tile_of % half == 1
+    high_all = jnp.where(upper, high_all[OTILE:, :], high_all[:OTILE, :]).astype(jnp.int32)
+    low_all = jnp.where(upper, low_all[OTILE:, :], low_all[:OTILE, :]).astype(jnp.int32)
+    wide = lax.broadcasted_iota(jnp.int32, (LANES, cells), 1)
+    firsts = [r * slots + t * FOOT for r in range(nr) for t in range(tiles_dev)]
+    firsts += [nr * slots + (tiles_dev + t) * FOOT for t in range(tiles_dev)]
+    for q, first in enumerate(firsts):
+        here = slice(q * LANES, (q + 1) * LANES)
+        high, low = [
+            jnp.concatenate([v[:, first + f : first + f + 1] for f in range(FOOT)], axis=0)
+            for v in (high_all, low_all)
+        ]
+        found = dot(jnp.where(lane == low, 1.0, 0.0).astype(BF16), table_t)
+        found = jnp.where(wide_lane % rows == high, found, 0.0).astype(BF16)
+        found = dot(found, collect)
+        feat[here, :] = found
+        hot[here, :] = jnp.where(wide == found[:, 0:1].astype(jnp.int32), 1.0, 0.0).astype(BF16)
+
+    for r in z_peers:
+        arrived(r, my_m)
+        for m in xy_peers:
+            send(r, my_m, (my_r, m))
+        send(r, my_m, (my_r, mate))
+    for r in [my_r] + z_peers:
+        for m in xy_peers:
+            arrived(r, m)
+            send(r, m, (my_r, mate))
+    mate_blocks = [mate] + [((chip + e) % chips) * CORES + (1 - core) for e in range(1, chips)]
+    for r in [my_r] + z_peers:
+        for m in mate_blocks:
+            arrived(r, m)
+
+    for r in range(nr):
+        turned = jnp.transpose(gathered[r])
+        state_t[r * cd : (r + 1) * cd, :] = turned
+        hi, lo = split2(turned)
+        parts[r * cd : (r + 1) * cd, :members] = hi
+        parts[r * cd : (r + 1) * cd, members:] = lo
+
+    firsts = nr * tiles_dev * STILE
+    both = dot(hot[:firsts, :], parts[...])
+    pert, step = obs_terms(
+        both[:, :members] + both[:, members:], feat[:firsts, 1:2], feat[:firsts, 2:3], members
+    )
+    pert_hi[...], pert_lo[...] = split2(pert)
+    step_hi[...], step_lo[...] = split2(step)
+
+    for r in range(nr):
+        for t in range(tiles_dev):
+            first = r * cd + t * STILE
+            obs = slice((r * tiles_dev + t) * STILE, (r * tiles_dev + t + 1) * STILE)
+            p_hi, p_lo, s_hi, s_lo = [ref[obs, :] for ref in (pert_hi, pert_lo, step_hi, step_lo)]
+            own = (parts[first : first + STILE, :members], parts[first : first + STILE, members:])
+            cov = dot3(own, (p_hi, p_lo), transposed=True)
+            new = state_t[first : first + STILE, :] + dot3(split2(cov), (s_hi, s_lo))
+            state_t[first : first + STILE, :] = new
+            hi, lo = split2(new)
+            parts[first : first + STILE, :members] = hi
+            parts[first : first + STILE, members:] = lo
+
+    for t in range(tiles_dev):
+        obs = slice(firsts + t * STILE, firsts + (t + 1) * STILE)
+        both = dot(hot[obs, :], parts[...])
+        pert, step = obs_terms(
+            both[:, :members] + both[:, members:], feat[obs, 1:2], feat[obs, 2:3], members
+        )
+        here = pl.ds(pl.multiple_of(my_r * cd + t * STILE, STILE), STILE)
+        cov = dot3((parts[here, :members], parts[here, members:]), split2(pert), transposed=True)
+        new = state_t[here, :] + dot3(split2(cov), split2(step))
+        final[:, t * STILE : (t + 1) * STILE] = jnp.transpose(new)
+    out_ref[...] = final[pl.ds(pl.multiple_of(my_m * md, md), md), :]
+
+    for copy in sent:
+        copy.wait_send()
+    for i, r in enumerate(z_peers):
+        fp_copy(i, my_r, r).wait_send()
+
+
+def replicated(nr, nm, ensemble, obs_value, obs_error, obs_region, obs_cell, order, footprint):
+    md, cd = ensemble.shape
+    members, cells = md * nm, cd * nr
+    total = order.shape[0]
+    lines = [v.reshape(total // LANES, LANES) for v in (order, obs_region, obs_cell, obs_error, obs_value)]
+    vmem = pl.BlockSpec(memory_space=pltpu.VMEM)
+    chips = nm // CORES
+    sends = (nr - 1) + nr * (chips - 1) + nr * chips
+    return pl.pallas_call(
+        functools.partial(kernel, nr, nm),
+        out_shape=jax.ShapeDtypeStruct((md, cd), F32),
+        in_specs=[pl.BlockSpec(memory_space=pltpu.SMEM)] + [vmem] * 6,
+        out_specs=vmem,
+        scratch_shapes=[
+            pltpu.VMEM((nr, members, cd), F32),
+            pltpu.VMEM((nr, 8, LANES), jnp.int32),
+            pltpu.VMEM((8, LANES), jnp.int32),
+            pltpu.VMEM((cells + cd, LANES), F32),
+            pltpu.VMEM((cells + cd, cells), BF16),
+            pltpu.VMEM((cells, members), F32),
+            pltpu.VMEM((cells, 2 * members), BF16),
+            pltpu.VMEM((cells, members), BF16),
+            pltpu.VMEM((cells, members), BF16),
+            pltpu.VMEM((cells, members), BF16),
+            pltpu.VMEM((cells, members), BF16),
+            pltpu.VMEM((members, cd), F32),
+            pltpu.SemaphoreType.DMA((sends,)),
+            pltpu.SemaphoreType.DMA((nr, nm)),
+            pltpu.SemaphoreType.DMA((nr,)),
+            pltpu.SemaphoreType.DMA((nr,)),
+        ],
+        compiler_params=pltpu.CompilerParams(
+            collective_id=0, has_side_effects=True, vmem_limit_bytes=48 * 1024 * 1024
+        ),
+    )(footprint, ensemble, *lines)
+
+
+def sharded(ensemble, obs_value, obs_error, obs_region, obs_cell, order, footprint):
     mem_dev, cell_count = ensemble.shape
     members = mem_dev * lax.axis_size("member")
     tile_count = cell_count // STILE
@@ -55,6 +326,13 @@
 
 
 def solution(mesh):
+    nr, nm = mesh.shape["region"], mesh.shape["member"]
+
+    def per_device(ensemble, *rest):
+        if 4 * ensemble.size * nr * nm <= REPLICATED_LIMIT:
+            return replicated(nr, nm, ensemble, *rest)
+        return sharded(ensemble, *rest)
+
     in_specs = (P("member", "region"), P(), P(), P(), P(), P(), P(None, "region", None))
     out_specs = P("member", "region")
     return jax.shard_map(

time: 253 us -> 31.5 us (0.12)
  the two profiles are of different devices: /device:TPU:0 before, /device:TPU:1 now
where the time goes in v1:
time: 31.5 us; the launch traced here: 31.1 us
  Pallas kernels  25.5 us (81%)
  local copies, waits for them, and re-layouts  5.54 us (18%)
    pallas_call x1, Pallas kernels, replicated(): pl.pallas_call(functools.partial(kernel, nr, nm), out_shape=jax.ShapeDtyp...  25.5 us
    unnamed x15, local copies, waits for them, and re-layouts  5.54 us

profile of v1, /device:TPU:1, one launch (start us, length us, event | category | flops | bytes accessed | tf_op | source)
XLA Modules:
  0.0 31.1 jit_solution(14201858309233011109)
XLA Ops:
  0.0 0.0 copy-start.1
  0.0 0.7 %copy-done.1 = s32[2048]{0:T(1024)S(1)} copy-done((s32[2048]{0:T(1024)S(1)}, s32[2048]{0:T(1024)}, u32[]{:S(2)}) %copy-start.1) | copy-done | bytes 8216
  0.7 0.0 copy-start
  0.7 0.8 %copy-done = f32[32,256]{1,0:T(8,128)S(1)} copy-done((f32[32,256]{1,0:T(8,128)S(1)}, f32[32,256]{1,0:T(8,128)}, u32[]{:S(2)}) %copy-start) | copy-done | bytes 32792
  1.5 0.0 copy-start.2
  1.5 0.7 %copy-done.2 = s32[2048]{0:T(1024)S(1)} copy-done((s32[2048]{0:T(1024)S(1)}, s32[2048]{0:T(1024)}, u32[]{:S(2)}) %copy-start.2) | copy-done | bytes 8216
  2.2 0.0 copy-start.3
  2.2 0.7 %copy-done.3 = s32[2048]{0:T(1024)S(1)} copy-done((s32[2048]{0:T(1024)S(1)}, s32[2048]{0:T(1024)}, u32[]{:S(2)}) %copy-start.3) | copy-done | bytes 8216
  2.9 0.0 copy-start.4
  2.9 0.7 %copy-done.4 = f32[2048]{0:T(1024)S(1)} copy-done((f32[2048]{0:T(1024)S(1)}, f32[2048]{0:T(1024)}, u32[]{:S(2)}) %copy-start.4) | copy-done | bytes 8216
  3.5 0.0 copy-start.5
  3.6 0.7 %copy-done.5 = f32[2048]{0:T(1024)S(1)} copy-done((f32[2048]{0:T(1024)S(1)}, f32[2048]{0:T(1024)}, u32[]{:S(2)}) %copy-start.5) | copy-done | bytes 8216
  4.2 0.0 copy-start.6
  4.2 0.7 %copy-done.6 = s32[2,2,2]{2,1,0:T(2,128)S(1)} copy-done((s32[2,2,2]{2,1,0:T(2,128)S(1)}, s32[2,2,2]{2,1,0:T(2,128)}, u32[]{:S(2)}) %copy-start.6) | copy-done | bytes 56
  4.9 25.5 %shard_map.73 = f32[32,256]{1,0:T(8,128)S(1)} custom-call(s32[2,2,2]{2,1,0:T(2,128)S(1)} %copy-done.6, f32[32,256]{1,0:T(8,128)S(1)} %copy-done, s32[16,128]{1,0:T(8,128)S(1)} %bitcast.5, s32[16,128]{1,0:T(8,128)S(1)} %bitcast.6, s32[16,128]{1,0:T(8,128)S(1)} %bitcast.7, f32[16,128]{1,0:T(8,128)S(1)} %bitcast.8, f32[16,128]{1,0:T(8,128)S(1)} %bitcast.9), custom_call_target="tpu_custom_call" | custom-call | tf_op jit(solution)/shard_map/pallas_call | solution.py:255
  30.5 0.6 %copy.9 = f32[32,256]{1,0:T(8,128)} copy(f32[32,256]{1,0:T(8,128)S(1)} %shard_map.73) | data formatting | bytes 65536
Async XLA Ops:
  0.0 0.7 %copy-start.1 = (s32[2048]{0:T(1024)S(1)}, s32[2048]{0:T(1024)}, u32[]{:S(2)}) copy-start(s32[2048]{0:T(1024)} %param.12) | copy-start | bytes 24580
  0.7 0.8 %copy-start = (f32[32,256]{1,0:T(8,128)S(1)}, f32[32,256]{1,0:T(8,128)}, u32[]{:S(2)}) copy-start(f32[32,256]{1,0:T(8,128)} %ens_ref.1) | copy-start | bytes 98308
  1.5 0.7 %copy-start.2 = (s32[2048]{0:T(1024)S(1)}, s32[2048]{0:T(1024)}, u32[]{:S(2)}) copy-start(s32[2048]{0:T(1024)} %param.10) | copy-start | bytes 24580
  2.2 0.7 %copy-start.3 = (s32[2048]{0:T(1024)S(1)}, s32[2048]{0:T(1024)}, u32[]{:S(2)}) copy-start(s32[2048]{0:T(1024)} %param.11) | copy-start | bytes 24580
  2.9 0.7 %copy-start.4 = (f32[2048]{0:T(1024)S(1)}, f32[2048]{0:T(1024)}, u32[]{:S(2)}) copy-start(f32[2048]{0:T(1024)} %param.9) | copy-start | bytes 24580
  3.5 0.7 %copy-start.5 = (f32[2048]{0:T(1024)S(1)}, f32[2048]{0:T(1024)}, u32[]{:S(2)}) copy-start(f32[2048]{0:T(1024)} %param.8) | copy-start | bytes 24580
  4.2 0.7 %copy-start.6 = (s32[2,2,2]{2,1,0:T(2,128)S(1)}, s32[2,2,2]{2,1,0:T(2,128)}, u32[]{:S(2)}) copy-start(s32[2,2,2]{2,1,0:T(2,128)} %fp_ref.1) | copy-start | bytes 100

commit v2 on v1

--- a/solution.py
+++ b/solution.py
@@ -56,12 +56,12 @@
 
 
 def kernel(
-    nr, nm, fp_ref, ens_ref, order_ref, region_ref, cell_ref, error_ref, value_ref, out_ref,
-    gathered, fp_all, fp_own, feat, hot, state_t, parts, pert_hi, pert_lo, step_hi, step_lo, final,
+    nr, nm, fp_hbm, ens_hbm, order_hbm, region_hbm, cell_hbm, error_hbm, value_hbm, out_ref,
+    fp_ref, order_ref, region_ref, cell_ref, error_ref, value_ref, load_sem, gathered, fp_all, fp_own, feat, hot, state_t, parts, pert_hi, pert_lo, step_hi, step_lo, final,
     send_sem, recv_sem, fp_send, fp_recv,
 ):
     my_r, my_m = lax.axis_index("region"), lax.axis_index("member")
-    md, cd = ens_ref.shape
+    md, cd = ens_hbm.shape
     members, cells = md * nm, cd * nr
     chips = nm // CORES
     chip, core = my_m // CORES, my_m % CORES
@@ -70,11 +70,29 @@
     z_peers = [(my_r + d) % nr for d in range(1, nr)]
     xy_peers = [((chip + e) % chips) * CORES + core for e in range(1, chips)]
 
+    own_block = gathered.at[my_r, pl.ds(pl.multiple_of(my_m * md, md), md), :]
+    loads = [
+        pltpu.make_async_copy(src, dst, load_sem.at[i])
+        for i, (src, dst) in enumerate(
+            [
+                (fp_hbm, fp_ref),
+                (ens_hbm, own_block),
+                (order_hbm, order_ref),
+                (region_hbm, region_ref),
+                (cell_hbm, cell_ref),
+                (error_hbm, error_ref),
+                (value_hbm, value_ref),
+            ]
+        )
+    ]
+    for load in loads:
+        load.start()
     barrier = pltpu.get_barrier_semaphore()
     for r in z_peers:
         pl.semaphore_signal(barrier, inc=1, device_id=(r, my_m), device_id_type=MESH)
     for m in xy_peers + [mate]:
         pl.semaphore_signal(barrier, inc=1, device_id=(my_r, m), device_id_type=MESH)
+    loads[0].wait()
     slots = BATCHES * tiles_dev * FOOT
     lane8 = lax.broadcasted_iota(jnp.int32, (8, LANES), 1)
     fp_sent, fp_here = [jnp.zeros((8, LANES), jnp.int32)] * 2
@@ -87,6 +105,7 @@
                 fp_here = jnp.where(lane8 == nr * slots + slot, tile, fp_here)
                 slot += 1
     fp_own[...] = fp_sent
+    loads[1].wait()
     pl.semaphore_wait(barrier, len(z_peers) + len(xy_peers) + 1)
 
     sent = []
@@ -94,9 +113,9 @@
     def block(r, m):
         return gathered.at[r, pl.ds(pl.multiple_of(m * md, md), md), :]
 
-    def send(r, m, to, own=False):
+    def send(r, m, to):
         copy = pltpu.make_async_remote_copy(
-            src_ref=ens_ref if own else block(r, m),
+            src_ref=block(r, m),
             dst_ref=block(r, m),
             send_sem=send_sem.at[len(sent)],
             recv_sem=recv_sem.at[r, m],
@@ -127,13 +146,14 @@
         )
 
     for r in z_peers:
-        send(my_r, my_m, (r, my_m), own=True)
+        send(my_r, my_m, (r, my_m))
     for m in xy_peers:
-        send(my_r, my_m, (my_r, m), own=True)
-    send(my_r, my_m, (my_r, mate), own=True)
+        send(my_r, my_m, (my_r, m))
+    send(my_r, my_m, (my_r, mate))
     for i, r in enumerate(z_peers):
         fp_copy(i, my_r, r).start()
-    gathered[my_r, pl.ds(pl.multiple_of(my_m * md, md), md), :] = ens_ref[...]
+    for load in loads[2:]:
+        load.wait()
 
     rows = order_ref.shape[0]
     table = jnp.concatenate(
@@ -249,15 +269,22 @@
     members, cells = md * nm, cd * nr
     total = order.shape[0]
     lines = [v.reshape(total // LANES, LANES) for v in (order, obs_region, obs_cell, obs_error, obs_value)]
-    vmem = pl.BlockSpec(memory_space=pltpu.VMEM)
+    line = (total // LANES, LANES)
     chips = nm // CORES
     sends = (nr - 1) + nr * (chips - 1) + nr * chips
     return pl.pallas_call(
         functools.partial(kernel, nr, nm),
         out_shape=jax.ShapeDtypeStruct((md, cd), F32),
-        in_specs=[pl.BlockSpec(memory_space=pltpu.SMEM)] + [vmem] * 6,
-        out_specs=vmem,
+        in_specs=[pl.BlockSpec(memory_space=pltpu.HBM)] * 7,
+        out_specs=pl.BlockSpec(memory_space=pltpu.VMEM),
         scratch_shapes=[
+            pltpu.SMEM(footprint.shape, jnp.int32),
+            pltpu.VMEM(line, jnp.int32),
+            pltpu.VMEM(line, jnp.int32),
+            pltpu.VMEM(line, jnp.int32),
+            pltpu.VMEM(line, F32),
+            pltpu.VMEM(line, F32),
+            pltpu.SemaphoreType.DMA((7,)),
             pltpu.VMEM((nr, members, cd), F32),
             pltpu.VMEM((nr, 8, LANES), jnp.int32),
             pltpu.VMEM((8, LANES), jnp.int32),
@@ -276,7 +303,7 @@
             pltpu.SemaphoreType.DMA((nr,)),
         ],
         compiler_params=pltpu.CompilerParams(
-            collective_id=0, has_side_effects=True, vmem_limit_bytes=48 * 1024 * 1024
+            collective_id=0, has_side_effects=True, vmem_limit_bytes=64 * 1024 * 1024
         ),
     )(footprint, ensemble, *lines)
 

time: 31.5 us -> 27.2 us (0.86)
  local copies, waits for them, and re-layouts: 5.54 us -> 1.38 us
    unnamed x15 -> x1, local copies, waits for them, and re-layouts: 5.54 us -> 1.38 us
where the time goes in v2:
time: 27.2 us; the launch traced here: 26.9 us
  Pallas kernels  25.5 us (94%)
  local copies, waits for them, and re-layouts  1.38 us (5%)
    pallas_call x1, Pallas kernels, replicated(): pl.pallas_call(functools.partial(kernel, nr, nm), out_shape=jax.ShapeDtyp...  25.5 us
    unnamed x1, local copies, waits for them, and re-layouts  1.38 us

profile of v2, /device:TPU:1, one launch (start us, length us, event | category | flops | bytes accessed | tf_op | source)
XLA Modules:
  0.0 26.9 jit_solution(11740970870950156879)
XLA Ops:
  0.0 25.5 %shard_map.73 = f32[32,256]{1,0:T(8,128)} custom-call(s32[2,2,2]{2,1,0:T(2,128)} %fp_hbm.1, f32[32,256]{1,0:T(8,128)} %ens_hbm.1, s32[16,128]{1,0:T(8,128)} %bitcast.5, s32[16,128]{1,0:T(8,128)} %bitcast.6, s32[16,128]{1,0:T(8,128)} %bitcast.7, f32[16,128]{1,0:T(8,128)} %bitcast.8, f32[16,128]{1,0:T(8,128)} %bitcast.9), custom_call_target="tpu_custom_call" | custom-call | tf_op jit(solution)/shard_map/pallas_call | solution.py:275
  25.5 1.4 %copy.9 = f32[32,256]{1,0:T(8,128)} copy(f32[32,256]{1,0:T(8,128)} %shard_map.73) | data formatting | bytes 65536

commit v3 on v2

--- a/solution.py
+++ b/solution.py
@@ -57,7 +57,7 @@
 
 def kernel(
     nr, nm, fp_hbm, ens_hbm, order_hbm, region_hbm, cell_hbm, error_hbm, value_hbm, out_ref,
-    fp_ref, order_ref, region_ref, cell_ref, error_ref, value_ref, load_sem, gathered, fp_all, fp_own, feat, hot, state_t, parts, pert_hi, pert_lo, step_hi, step_lo, final,
+    fp_ref, order_ref, region_ref, cell_ref, error_ref, value_ref, load_sem, gathered, fp_all, fp_own, feat, hot, priors, state_t, parts, pert_hi, pert_lo, step_hi, step_lo, final,
     send_sem, recv_sem, fp_send, fp_recv,
 ):
     my_r, my_m = lax.axis_index("region"), lax.axis_index("member")
@@ -67,7 +67,7 @@
     chip, core = my_m // CORES, my_m % CORES
     mate = chip * CORES + (1 - core)
     tiles_dev = cd // STILE
-    z_peers = [(my_r + d) % nr for d in range(1, nr)]
+    z_peers = [(my_r + d) % nr for d in sorted(range(1, nr), key=lambda d: min(d, nr - d))]
     xy_peers = [((chip + e) % chips) * CORES + core for e in range(1, chips)]
 
     own_block = gathered.at[my_r, pl.ds(pl.multiple_of(my_m * md, md), md), :]
@@ -209,27 +209,33 @@
         for m in xy_peers:
             send(r, my_m, (my_r, m))
         send(r, my_m, (my_r, mate))
-    for r in [my_r] + z_peers:
+    mate_blocks = [mate] + [((chip + e) % chips) * CORES + (1 - core) for e in range(1, chips)]
+    first_obs = nr * tiles_dev * STILE
+
+    def take_in(i, r):
+        for m in mate_blocks:
+            arrived(r, m)
+        here = pl.ds(pl.multiple_of(r * cd, cd), cd)
+        turned = jnp.transpose(gathered[r])
+        state_t[here, :] = turned
+        hi, lo = split2(turned)
+        parts[here, :members] = hi
+        parts[here, members:] = lo
+        mine = hot[:first_obs, here]
+        partial = dot(mine, hi) + dot(mine, lo)
+        priors[...] = partial if i == 0 else priors[...] + partial
+
+    regions = [my_r] + z_peers
+    for i, r in enumerate(regions):
         for m in xy_peers:
             arrived(r, m)
             send(r, m, (my_r, mate))
-    mate_blocks = [mate] + [((chip + e) % chips) * CORES + (1 - core) for e in range(1, chips)]
-    for r in [my_r] + z_peers:
-        for m in mate_blocks:
-            arrived(r, m)
-
-    for r in range(nr):
-        turned = jnp.transpose(gathered[r])
-        state_t[r * cd : (r + 1) * cd, :] = turned
-        hi, lo = split2(turned)
-        parts[r * cd : (r + 1) * cd, :members] = hi
-        parts[r * cd : (r + 1) * cd, members:] = lo
-
-    firsts = nr * tiles_dev * STILE
-    both = dot(hot[:firsts, :], parts[...])
-    pert, step = obs_terms(
-        both[:, :members] + both[:, members:], feat[:firsts, 1:2], feat[:firsts, 2:3], members
-    )
+        if i > 0:
+            take_in(i - 1, regions[i - 1])
+    take_in(nr - 1, regions[-1])
+
+    firsts = first_obs
+    pert, step = obs_terms(priors[...], feat[:firsts, 1:2], feat[:firsts, 2:3], members)
     pert_hi[...], pert_lo[...] = split2(pert)
     step_hi[...], step_lo[...] = split2(step)
 
@@ -291,6 +297,7 @@
             pltpu.VMEM((cells + cd, LANES), F32),
             pltpu.VMEM((cells + cd, cells), BF16),
             pltpu.VMEM((cells, members), F32),
+            pltpu.VMEM((cells, members), F32),
             pltpu.VMEM((cells, 2 * members), BF16),
             pltpu.VMEM((cells, members), BF16),
             pltpu.VMEM((cells, members), BF16),

time: 27.2 us -> 25.5 us (0.938)
  the two profiles are of different devices: /device:TPU:1 before, /device:TPU:0 now
where the time goes in v3:
time: 25.5 us; the launch traced here: 25.2 us
  Pallas kernels  23.9 us (94%)
  local copies, waits for them, and re-layouts  1.38 us (5%)
    pallas_call x1, Pallas kernels, replicated(): pl.pallas_call(functools.partial(kernel, nr, nm), out_shape=jax.ShapeDtyp...  23.9 us
    unnamed x1, local copies, waits for them, and re-layouts  1.38 us

profile of v3, /device:TPU:0, one launch (start us, length us, event | category | flops | bytes accessed | tf_op | source)
XLA Modules:
  0.0 25.2 jit_solution(6661700924093709231)
XLA Ops:
  0.0 23.9 %shard_map.73 = f32[32,256]{1,0:T(8,128)} custom-call(s32[2,2,2]{2,1,0:T(2,128)} %fp_hbm.1, f32[32,256]{1,0:T(8,128)} %ens_hbm.1, s32[16,128]{1,0:T(8,128)} %bitcast.5, s32[16,128]{1,0:T(8,128)} %bitcast.6, s32[16,128]{1,0:T(8,128)} %bitcast.7, f32[16,128]{1,0:T(8,128)} %bitcast.8, f32[16,128]{1,0:T(8,128)} %bitcast.9), custom_call_target="tpu_custom_call" | custom-call | tf_op jit(solution)/shard_map/pallas_call | solution.py:281
  23.9 1.4 %copy.9 = f32[32,256]{1,0:T(8,128)} copy(f32[32,256]{1,0:T(8,128)} %shard_map.73) | data formatting | bytes 65536

commit v4 on v3

--- a/solution.py
+++ b/solution.py
@@ -310,9 +310,9 @@
             pltpu.SemaphoreType.DMA((nr,)),
         ],
         compiler_params=pltpu.CompilerParams(
-            collective_id=0, has_side_effects=True, vmem_limit_bytes=64 * 1024 * 1024
+            collective_id=0, has_side_effects=True, vmem_limit_bytes=48 * 1024 * 1024
         ),
-    )(footprint, ensemble, *lines)
+    )(*[pltpu.with_memory_space_constraint(v, pltpu.HBM) for v in (footprint, ensemble, *lines)])
 
 
 def sharded(ensemble, obs_value, obs_error, obs_region, obs_cell, order, footprint):

time: 25.5 us -> 24.1 us (0.945)
  local copies, waits for them, and re-layouts: 1.38 us -> 0.62 us
  Pallas kernels: 23.9 us -> 23.3 us
    unnamed x1, local copies, waits for them, and re-layouts: 1.38 us -> 0.62 us
    pallas_call x1, Pallas kernels: 23.9 us -> 23.3 us  [replicated(): pl.pallas_call(functools.partial(kernel, nr, nm), out_shape=jax.ShapeDtyp...]
where the time goes in v4:
time: 24.1 us; the launch traced here: 23.9 us
  Pallas kernels  23.3 us (97%)
  local copies, waits for them, and re-layouts  0.62 us (3%)
    pallas_call x1, Pallas kernels, replicated(): pl.pallas_call(functools.partial(kernel, nr, nm), out_shape=jax.ShapeDtyp...  23.3 us
    unnamed x1, local copies, waits for them, and re-layouts  0.62 us

profile of v4, /device:TPU:0, one launch (start us, length us, event | category | flops | bytes accessed | tf_op | source)
XLA Modules:
  0.0 23.9 jit_solution(15656037301422061238)
XLA Ops:
  0.0 23.3 %shard_map.73 = f32[32,256]{1,0:T(8,128)S(1)} custom-call(s32[2,2,2]{2,1,0:T(2,128)} %fp_hbm.1, f32[32,256]{1,0:T(8,128)} %ens_hbm.1, s32[16,128]{1,0:T(8,128)} %bitcast.5, s32[16,128]{1,0:T(8,128)} %bitcast.6, s32[16,128]{1,0:T(8,128)} %bitcast.7, f32[16,128]{1,0:T(8,128)} %bitcast.8, f32[16,128]{1,0:T(8,128)} %bitcast.9), custom_call_target="tpu_custom_call" | custom-call | tf_op jit(solution)/shard_map/pallas_call | solution.py:281
  23.3 0.6 %copy.9 = f32[32,256]{1,0:T(8,128)} copy(f32[32,256]{1,0:T(8,128)S(1)} %shard_map.73) | data formatting | bytes 65536

commit v5 on v4

--- a/solution.py
+++ b/solution.py
@@ -45,12 +45,13 @@
     return dot(a_hi, b_hi, transposed) + (dot(a_hi, b_lo, transposed) + dot(a_lo, b_hi, transposed))
 
 
-def obs_terms(priors, err, val, members):
+def obs_terms(priors, err, val, err_root, members):
     mean = jnp.sum(priors, axis=1, keepdims=True) * (1.0 / members)
     pert = priors - mean
     var = jnp.sum(pert * pert, axis=1, keepdims=True) * (1.0 / (members - 1))
-    gain = 1.0 / (var + err)
-    shrink = 1.0 / (1.0 + jnp.sqrt(err * gain))
+    root = lax.rsqrt(var + err)
+    gain = root * root
+    shrink = 1.0 / (1.0 + err_root * root)
     step = (gain * (1.0 / (members - 1))) * ((val - mean) - shrink * pert)
     return pert, step
 
@@ -201,7 +202,7 @@
         found = dot(jnp.where(lane == low, 1.0, 0.0).astype(BF16), table_t)
         found = jnp.where(wide_lane % rows == high, found, 0.0).astype(BF16)
         found = dot(found, collect)
-        feat[here, :] = found
+        feat[here, :] = jnp.where(lane == 3, jnp.sqrt(found[:, 1:2]), found)
         hot[here, :] = jnp.where(wide == found[:, 0:1].astype(jnp.int32), 1.0, 0.0).astype(BF16)
 
     for r in z_peers:
@@ -235,7 +236,7 @@
     take_in(nr - 1, regions[-1])
 
     firsts = first_obs
-    pert, step = obs_terms(priors[...], feat[:firsts, 1:2], feat[:firsts, 2:3], members)
+    pert, step = obs_terms(priors[...], feat[:firsts, 1:2], feat[:firsts, 2:3], feat[:firsts, 3:4], members)
     pert_hi[...], pert_lo[...] = split2(pert)
     step_hi[...], step_lo[...] = split2(step)
 
@@ -256,7 +257,7 @@
         obs = slice(firsts + t * STILE, firsts + (t + 1) * STILE)
         both = dot(hot[obs, :], parts[...])
         pert, step = obs_terms(
-            both[:, :members] + both[:, members:], feat[obs, 1:2], feat[obs, 2:3], members
+            both[:, :members] + both[:, members:], feat[obs, 1:2], feat[obs, 2:3], feat[obs, 3:4], members
         )
         here = pl.ds(pl.multiple_of(my_r * cd + t * STILE, STILE), STILE)
         cov = dot3((parts[here, :members], parts[here, members:]), split2(pert), transposed=True)

time: 24.1 us -> 24.6 us (1.021)
  Pallas kernels: 23.3 us -> 23.8 us
    pallas_call x1, Pallas kernels: 23.3 us -> 23.8 us  [replicated(): pl.pallas_call(functools.partial(kernel, nr, nm), out_shape=jax.ShapeDtyp...]
where the time goes in v5:
time: 24.6 us; the launch traced here: 24.4 us
  Pallas kernels  23.8 us (97%)
  local copies, waits for them, and re-layouts  0.62 us (3%)
    pallas_call x1, Pallas kernels, replicated(): pl.pallas_call(functools.partial(kernel, nr, nm), out_shape=jax.ShapeDtyp...  23.8 us
    unnamed x1, local copies, waits for them, and re-layouts  0.62 us

profile of v5, /device:TPU:0, one launch (start us, length us, event | category | flops | bytes accessed | tf_op | source)
XLA Modules:
  0.0 24.4 jit_solution(11819167896733020425)
XLA Ops:
  0.0 23.8 %shard_map.73 = f32[32,256]{1,0:T(8,128)S(1)} custom-call(s32[2,2,2]{2,1,0:T(2,128)} %fp_hbm.1, f32[32,256]{1,0:T(8,128)} %ens_hbm.1, s32[16,128]{1,0:T(8,128)} %bitcast.5, s32[16,128]{1,0:T(8,128)} %bitcast.6, s32[16,128]{1,0:T(8,128)} %bitcast.7, f32[16,128]{1,0:T(8,128)} %bitcast.8, f32[16,128]{1,0:T(8,128)} %bitcast.9), custom_call_target="tpu_custom_call" | custom-call | tf_op jit(solution)/shard_map/pallas_call | solution.py:282
  23.8 0.6 %copy.9 = f32[32,256]{1,0:T(8,128)} copy(f32[32,256]{1,0:T(8,128)S(1)} %shard_map.73) | data formatting | bytes 65536

commit v6 on v4

--- a/solution.py
+++ b/solution.py
@@ -42,7 +42,9 @@
 def dot3(a, b, transposed=False):
     a_hi, a_lo = a
     b_hi, b_lo = b
-    return dot(a_hi, b_hi, transposed) + (dot(a_hi, b_lo, transposed) + dot(a_lo, b_hi, transposed))
+    left = jnp.concatenate([a_hi, a_hi, a_lo], axis=1)
+    right = jnp.concatenate([b_hi, b_lo, b_hi], axis=1 if transposed else 0)
+    return dot(left, right, transposed)
 
 
 def obs_terms(priors, err, val, members):

time: 24.1 us -> 23.7 us (0.983)
  Pallas kernels: 23.3 us -> 22.9 us
    pallas_call x1, Pallas kernels: 23.3 us -> 22.9 us  [replicated(): pl.pallas_call(functools.partial(kernel, nr, nm), out_shape=jax.ShapeDtyp...]
where the time goes in v6:
time: 23.7 us; the launch traced here: 23.6 us
  Pallas kernels  22.9 us (97%)
  local copies, waits for them, and re-layouts  0.62 us (3%)
    pallas_call x1, Pallas kernels, replicated(): pl.pallas_call(functools.partial(kernel, nr, nm), out_shape=jax.ShapeDtyp...  22.9 us
    unnamed x1, local copies, waits for them, and re-layouts  0.62 us

profile of v6, /device:TPU:0, one launch (start us, length us, event | category | flops | bytes accessed | tf_op | source)
XLA Modules:
  0.0 23.6 jit_solution(1142748496481338078)
XLA Ops:
  0.0 22.9 %shard_map.73 = f32[32,256]{1,0:T(8,128)S(1)} custom-call(s32[2,2,2]{2,1,0:T(2,128)} %fp_hbm.1, f32[32,256]{1,0:T(8,128)} %ens_hbm.1, s32[16,128]{1,0:T(8,128)} %bitcast.5, s32[16,128]{1,0:T(8,128)} %bitcast.6, s32[16,128]{1,0:T(8,128)} %bitcast.7, f32[16,128]{1,0:T(8,128)} %bitcast.8, f32[16,128]{1,0:T(8,128)} %bitcast.9), custom_call_target="tpu_custom_call" | custom-call | tf_op jit(solution)/shard_map/pallas_call | solution.py:283
  23.0 0.6 %copy.9 = f32[32,256]{1,0:T(8,128)} copy(f32[32,256]{1,0:T(8,128)S(1)} %shard_map.73) | data formatting | bytes 65536
